TPU v7x, 32 devices: a whole 2x2x4 slice. The times are simulated.
32 devices in a mesh: row: 4 (over z), col: 8 (over y, x, core).
Axes of the slice: x: 2, y: 2, z: 4, core: 2. Of those that a mesh axis runs over, the one named last changes fastest.
Arguments:
- unfolding: bfloat16 [3072, 4096], P('row', 'col'), may hold values from -400 to 400
Outputs:
- regrouped: bfloat16 [256, 16, 3072], P('col', None, 'row')
All inputs are finite; a program needn't handle non-finite values.
Results may differ from a plain program's by a relative error of at most 0.0062.
Values may be sent and summed in bfloat16 or wider, within the bound.
A program may use at most 64 MiB of HBM per device.

v0:
```python
import math

import jax
import jax.numpy as jnp
from jax import lax
from jax.sharding import PartitionSpec as P

PIXELS = 256
ITERS = 2
COLS = 4096


def local(unfolding):
    rows_dev = unfolding.shape[0]
    cols_dev = unfolding.shape[1]
    total_rows = rows_dev * lax.axis_size("row")
    values = unfolding.astype(jnp.float32)
    sumsq = lax.psum(jnp.sum(values * values), ("row", "col"))
    factor = math.sqrt(COLS) / (3.0 * jnp.sqrt(sumsq))
    current = (values * factor).astype(jnp.bfloat16)
    updated = current.astype(jnp.float32)
    for turn_index in range(ITERS):
        gathered = lax.all_gather(current, "col", axis=1, tiled=True)
        partial_gram = lax.dot_general(
            current, gathered, (((0,), (0,)), ((), ())), preferred_element_type=jnp.float32
        )
        shares = lax.psum_scatter(partial_gram, "row", scatter_dimension=1, tiled=True).astype(
            jnp.bfloat16
        )
        gram_rows = lax.all_gather(shares, "row", axis=1, tiled=True)
        first = lax.dot_general(
            gathered, gram_rows, (((1,), (1,)), ((), ())), preferred_element_type=jnp.float32
        ).astype(jnp.bfloat16)
        second = lax.dot_general(
            lax.all_gather(first, "col", axis=1, tiled=True),
            gram_rows,
            (((1,), (1,)), ((), ())),
            preferred_element_type=jnp.float32,
        )
        updated = (
            1.875 * current.astype(jnp.float32) - 1.25 * first.astype(jnp.float32) + 0.375 * second
        )
        if turn_index + 1 < ITERS:
            current = updated.astype(jnp.bfloat16)
    final = updated * math.sqrt(total_rows)
    view_count = cols_dev // PIXELS
    cube = final.reshape(rows_dev, view_count, PIXELS).transpose(2, 1, 0).astype(jnp.bfloat16)
    return lax.all_to_all(cube, "col", split_axis=0, concat_axis=1, tiled=True)


def solution(mesh):
    return jax.shard_map(
        local,
        mesh=mesh,
        in_specs=(P("row", "col"),),
        out_specs=P("col", None, "row"),
        check_vma=False,
    )
```

profile of v0, /device:TPU:0, one launch (start us, length us, event | category | flops | bytes accessed | tf_op | source)
XLA Modules:
  0.0 767.1 jit_solution(5012271120336525755)
XLA Ops:
  6.5 0.0 all-gather.7.cloned.1.call-start
  6.5 1.4 copy.4
  7.9 1.0 fusion
  9.0 42.2 %psum.7 = f32[]{:T(128)} all-reduce(f32[]{:T(128)} %fusion), channel_id=1, replica_groups=mesh['row'=4,'col'=8] {'row','col'}, use_global_device_ids=true, to_apply=%region_1.0 | all-reduce | flops 1 | bytes 8 | tf_op jit(solution)/shard_map/psum | solution.py:18
  51.8 1.0 fusion.1
  52.9 0.0 all-gather.7.cloned.1.call-update
  52.9 0.0 reduce-scatter.3.cloned.1.call-start
  52.9 45.5 %all-gather.7.cloned.1.call-done = bf16[768,4096]{0,1:T(8,128)(2,1)} async-done(((bf16[768,512]{0,1:T(8,128)(2,1)}), bf16[768,4096]{0,1:T(8,128)(2,1)}) %all-gather.7.cloned.1.call-update) | async-done | bytes 6291472 | tf_op jit(solution)/shard_map/all_gather | solution.py:23
  98.4 9.7 %fusion.2 = f32[512,4096]{1,0:T(8,128)} fusion(bf16[768,512]{0,1:T(8,128)(2,1)} %fusion.1, bf16[768,4096]{0,1:T(8,128)(2,1)} %all-gather.7.cloned.1.call-done), kind=kOutput, calls=%fused_computation.9 | convolution fusion | flops 3221225472 | bytes 15466496 | tf_op jit(solution)/shard_map/dot_general | solution.py:24
  108.2 0.0 reduce-scatter.3.cloned.1.call-update
  108.2 0.0 all-gather.9.cloned.1.call-start
  108.2 144.7 %reduce-scatter.3.cloned.1.call-done = f32[512,1024]{1,0:T(8,128)} async-done(((f32[512,4096]{1,0:T(8,128)}), f32[512,1024]{1,0:T(8,128)}) %reduce-scatter.3.cloned.1.call-update) | async-done | bytes 2097168 | tf_op jit(solution)/shard_map/reduce_scatter | solution.py:27
  253.0 2.7 convert_element_type.45
  255.7 0.0 all-gather.9.cloned.1.call-update
  255.7 0.0 copy-start
  255.7 0.0 all-gather.11.cloned.1.call-start
  255.8 81.4 %all-gather.9.cloned.1.call-done = bf16[512,4096]{1,0:T(8,128)(2,1)} async-done(((bf16[512,1024]{1,0:T(8,128)(2,1)}), bf16[512,4096]{1,0:T(8,128)(2,1)}) %all-gather.9.cloned.1.call-update) | async-done | bytes 4194320 | tf_op jit(solution)/shard_map/all_gather | solution.py:30
  337.2 8.4 %convolution_convert_fusion.1 = bf16[768,512]{0,1:T(8,128)(2,1)} fusion(bf16[512,4096]{1,0:T(8,128)(2,1)} %all-gather.9.cloned.1.call-done, bf16[768,4096]{0,1:T(8,128)(2,1)} %all-gather.7.cloned.1.call-done), kind=kOutput, calls=%fused_computation.7 | convolution fusion | flops 3221618688 | bytes 11272192 | tf_op jit(solution)/shard_map/dot_general | solution.py:31
  345.6 0.0 all-gather.11.cloned.1.call-update
  345.6 0.0 all-gather.13.cloned.1.call-start
  345.7 44.0 %all-gather.11.cloned.1.call-done = bf16[768,4096]{0,1:T(8,128)(2,1)} async-done(((bf16[768,512]{0,1:T(8,128)(2,1)}), bf16[768,4096]{0,1:T(8,128)(2,1)}) %all-gather.11.cloned.1.call-update) | async-done | bytes 6291472 | tf_op jit(solution)/shard_map/all_gather | solution.py:35
  389.6 0.0 copy-done
  389.6 8.5 %add_convert_fusion = bf16[768,512]{0,1:T(8,128)(2,1)} fusion(bf16[768,512]{0,1:T(8,128)(2,1)} %convolution_convert_fusion.1, bf16[768,512]{0,1:T(8,128)(2,1)S(1)} %copy-done, bf16[512,4096]{1,0:T(8,128)(2,1)} %all-gather.9.cloned.1.call-done, bf16[768,4096]{0,1:T(8,128)(2,1)} %all-gather.11.cloned.1.call-done), kind=kOutput, calls=%fused_computation.5 | convolution fusion | flops 3224371200 | bytes 12845056 | tf_op jit(solution)/shard_map/dot_general | solution.py:34
  398.2 0.0 all-gather.13.cloned.1.call-update
  398.2 0.2 reduce-scatter.5.cloned.1.call-start
  398.4 45.3 %all-gather.13.cloned.1.call-done = bf16[768,4096]{0,1:T(8,128)(2,1)} async-done(((bf16[768,512]{0,1:T(8,128)(2,1)}), bf16[768,4096]{0,1:T(8,128)(2,1)}) %all-gather.13.cloned.1.call-update) | async-done | bytes 6291472 | tf_op jit(solution)/shard_map/all_gather | solution.py:23
  443.7 9.7 %fusion.3 = f32[512,4096]{1,0:T(8,128)} fusion(bf16[768,512]{0,1:T(8,128)(2,1)} %add_convert_fusion, bf16[768,4096]{0,1:T(8,128)(2,1)} %all-gather.13.cloned.1.call-done), kind=kOutput, calls=%fused_computation.10 | convolution fusion | flops 3221225472 | bytes 15466496 | tf_op jit(solution)/shard_map/dot_general | solution.py:24
  453.5 0.0 reduce-scatter.5.cloned.1.call-update
  453.5 0.0 all-gather.15.cloned.1.call-start
  453.6 144.7 %reduce-scatter.5.cloned.1.call-done = f32[512,1024]{1,0:T(8,128)} async-done(((f32[512,4096]{1,0:T(8,128)}), f32[512,1024]{1,0:T(8,128)}) %reduce-scatter.5.cloned.1.call-update) | async-done | bytes 2097168 | tf_op jit(solution)/shard_map/reduce_scatter | solution.py:27
  598.3 2.7 convert_element_type.50
  601.0 0.0 all-gather.15.cloned.1.call-update
  601.0 0.0 copy-start.1
  601.1 0.0 all-gather.17.cloned.1.call-start
  601.1 81.4 %all-gather.15.cloned.1.call-done = bf16[512,4096]{1,0:T(8,128)(2,1)} async-done(((bf16[512,1024]{1,0:T(8,128)(2,1)}), bf16[512,4096]{1,0:T(8,128)(2,1)}) %all-gather.15.cloned.1.call-update) | async-done | bytes 4194320 | tf_op jit(solution)/shard_map/all_gather | solution.py:30
  682.5 8.4 %convolution_convert_fusion = bf16[768,512]{0,1:T(8,128)(2,1)} fusion(bf16[512,4096]{1,0:T(8,128)(2,1)} %all-gather.15.cloned.1.call-done, bf16[768,4096]{0,1:T(8,128)(2,1)} %all-gather.13.cloned.1.call-done), kind=kOutput, calls=%fused_computation.6 | convolution fusion | flops 3221618688 | bytes 11272192 | tf_op jit(solution)/shard_map/dot_general | solution.py:31
  690.9 0.0 all-gather.17.cloned.1.call-update
  690.9 44.0 %all-gather.17.cloned.1.call-done = bf16[768,4096]{0,1:T(8,128)(2,1)} async-done(((bf16[768,512]{0,1:T(8,128)(2,1)}), bf16[768,4096]{0,1:T(8,128)(2,1)}) %all-gather.17.cloned.1.call-update) | async-done | bytes 6291472 | tf_op jit(solution)/shard_map/all_gather | solution.py:35
  735.0 0.0 copy-done.1
  735.0 7.7 multiply_convert_fusion
  742.6 0.8 copy.8
  743.4 15.1 %all_to_all.18 = bf16[256,2,768]{2,1,0:T(2,128)(2,1)S(1)} all-to-all(bf16[256,2,768]{2,1,0:T(2,128)(2,1)S(1)} %bitcast.19), channel_id=1, replica_groups=mesh['row'=4,'col'=8] {'col'}, dimensions={0} | all-to-all | bytes 1572864 | tf_op jit(solution)/shard_map/all_to_all | solution.py:48
  758.5 0.5 copy.6
  759.1 1.2 all_to_all.16
Async XLA Ops:
  6.5 91.9 %all-gather.7.cloned.1.call-start = ((), (), s32[]{:S(2)}) async-start(), calls=%async_computation.3 | async-start | bytes 7077888 | tf_op jit(solution)/shard_map/all_gather | solution.py:23
  52.9 200.1 %reduce-scatter.3.cloned.1.call-start = ((), (), s32[]{:S(2)}) async-start(), calls=%async_computation.4 | async-start | bytes 10485760 | tf_op jit(solution)/shard_map/reduce_scatter | solution.py:27
  108.2 229.0 %all-gather.9.cloned.1.call-start = ((), (), s32[]{:S(2)}) async-start(), calls=%async_computation.5 | async-start | bytes 5242880 | tf_op jit(solution)/shard_map/all_gather | solution.py:30
  255.7 133.9 %copy-start = (bf16[768,512]{0,1:T(8,128)(2,1)S(1)}, bf16[768,512]{0,1:T(8,128)(2,1)}, u32[]{:S(2)}) copy-start(bf16[768,512]{0,1:T(8,128)(2,1)} %fusion.1) | copy-start | bytes 2359300
  255.7 133.9 %all-gather.11.cloned.1.call-start = ((), (), s32[]{:S(2)}) async-start(), calls=%async_computation.6 | async-start | bytes 7077888 | tf_op jit(solution)/shard_map/all_gather | solution.py:35
  345.6 98.1 %all-gather.13.cloned.1.call-start = ((), (), s32[]{:S(2)}) async-start(), calls=%async_computation.7 | async-start | bytes 7077888 | tf_op jit(solution)/shard_map/all_gather | solution.py:23
  398.2 200.1 %reduce-scatter.5.cloned.1.call-start = ((), (), s32[]{:S(2)}) async-start(), calls=%async_computation.8 | async-start | bytes 10485760 | tf_op jit(solution)/shard_map/reduce_scatter | solution.py:27
  453.5 229.0 %all-gather.15.cloned.1.call-start = ((), (), s32[]{:S(2)}) async-start(), calls=%async_computation.9 | async-start | bytes 5242880 | tf_op jit(solution)/shard_map/all_gather | solution.py:30
  601.0 133.9 %copy-start.1 = (bf16[768,512]{0,1:T(8,128)(2,1)S(1)}, bf16[768,512]{0,1:T(8,128)(2,1)}, u32[]{:S(2)}) copy-start(bf16[768,512]{0,1:T(8,128)(2,1)} %add_convert_fusion) | copy-start | bytes 2359300
  601.1 133.9 %all-gather.17.cloned.1.call-start = ((), (), s32[]{:S(2)}) async-start(), calls=%async_computation.10 | async-start | bytes 7077888 | tf_op jit(solution)/shard_map/all_gather | solution.py:35
Sparse Core Ops, SparseCore 0:
  53.0 45.3 all-gather.6
  108.3 144.6 reduce-scatter.2
  255.8 81.3 all-gather.8
  345.7 43.8 all-gather.10
  398.3 45.3 all-gather.12
  453.6 144.6 reduce-scatter.4
  601.2 81.3 all-gather.14
  691.0 43.8 all-gather.16
where the time goes:
time: 767 us
  waiting for transfers between devices  631 us (82%)
  blocking collectives  57.2 us (7%)
  matrix products  52.4 us (7%)
  between operations  14.3 us (2%)
    reduce_scatter x2, waiting for transfers between devices, local(): lax.psum_scatter(partial_gram, 'row', scatter_dimension=1, tiled=True)  289 us
    all_gather x2, waiting for transfers between devices, local(): gram_rows = lax.all_gather(shares, 'row', axis=1, tiled=True)  163 us
    all_gather x2, waiting for transfers between devices, local(): gathered = lax.all_gather(current, 'col', axis=1, tiled=True)  90.8 us
    all_gather x2, waiting for transfers between devices, local(): lax.all_gather(first, 'col', axis=1, tiled=True)  88 us
    psum x1, blocking collectives, local(): sumsq = lax.psum(jnp.sum(values * values), ('row', 'col'))  42.2 us
    dot_general x2, matrix products, local(): lax.dot_general(current, gathered, (((0,), (0,)), ((), ())), preferred_el...  19.5 us
    dot_general x2, matrix products, local(): lax.dot_general(gathered, gram_rows, (((1,), (1,)), ((), ())), preferred_...  16.7 us
    dot_general x2, matrix products, local(): lax.dot_general(lax.all_gather(first, 'col', axis=1, tiled=True), gram_ro...  16.2 us
  transfers between devices with their start and end apart: 8, of which 8 were waited for; matrix products, arithmetic and copies ran while one was open for 0% of the time, Pallas kernels for 0%

commit v1 on v0

--- a/solution.py
+++ b/solution.py
@@ -1,16 +1,232 @@
+import functools
 import math
 
 import jax
 import jax.numpy as jnp
 from jax import lax
+from jax.experimental import pallas as pl
+from jax.experimental.pallas import tpu as pltpu
 from jax.sharding import PartitionSpec as P
 
 PIXELS = 256
 ITERS = 2
 COLS = 4096
-
-
-def local(unfolding):
+MESH = pl.DeviceIdType.MESH
+
+
+def exchange(nr, nc, x_ref, h_ref, xd_ref, ss_ref, xg, part, sendb, recvb, ssg,
+             own_sem, a_s, a_r, b_s, b_r, d_s, d_r, s_s, s_r, f_s, f_r, g_s, g_r):
+    r = lax.axis_index("row")
+    c = lax.axis_index("col")
+    rd = x_ref.shape[0]
+    w = x_ref.shape[1] // nr
+    st = part.shape[0]
+    ch = st // nr
+    direct = tuple(range(2, nc, 2))
+
+    barrier = pltpu.get_barrier_semaphore()
+    for k in range(1, nr):
+        pl.semaphore_signal(barrier, inc=1, device_id=(lax.rem(r + k, nr), c), device_id_type=MESH)
+    for d in (1,) + direct:
+        pl.semaphore_signal(barrier, inc=1, device_id=(r, c ^ d), device_id_type=MESH)
+    pl.semaphore_wait(barrier, nr - 1 + 1 + len(direct))
+
+    def lanes(index):
+        return pl.ds(pl.multiple_of(index * w, w), w)
+
+    def rows(index, size):
+        return pl.ds(pl.multiple_of(index * size, size), size)
+
+    def to_row(src, dst, s_sem, r_sem, k):
+        return pltpu.make_async_remote_copy(
+            src_ref=src, dst_ref=dst, send_sem=s_sem, recv_sem=r_sem,
+            device_id=(lax.rem(r + k, nr), c), device_id_type=MESH)
+
+    def to_col(src, dst, s_sem, r_sem, d):
+        return pltpu.make_async_remote_copy(
+            src_ref=src, dst_ref=dst, send_sem=s_sem, recv_sem=r_sem,
+            device_id=(r, c ^ d), device_id_type=MESH)
+
+    def gather_col(view, s_sem, r_sem, ready):
+        copies = {}
+
+        def send(k, piece, slot, d):
+            ref = view(k, piece)
+            copies[k, slot] = to_col(ref, ref, s_sem.at[k, slot], r_sem.at[k, slot], d)
+            copies[k, slot].start()
+
+        for k in range(nr):
+            ready(k)
+            for d in direct + (1,):
+                send(k, c, d, d)
+        for k in range(nr):
+            for d in direct:
+                copies[k, d].wait_recv()
+                send(k, c ^ d, d ^ 1, 1)
+        for k in range(nr):
+            for d in range(1, nc, 2):
+                copies[k, d].wait_recv()
+        for key in copies:
+            copies[key].wait_send()
+
+    a = {}
+    for k in range(1, nr):
+        a[k] = to_row(x_ref.at[:, lanes(lax.rem(r + k, nr))], xg.at[rows(r, rd), lanes(c)],
+                      a_s.at[k], a_r.at[k], k)
+        a[k].start()
+    own = pltpu.make_async_copy(x_ref.at[:, lanes(r)], xg.at[rows(r, rd), lanes(c)], own_sem)
+    own.start()
+
+    def ready_x(k):
+        if k == 0:
+            own.wait()
+        else:
+            a[k].wait_recv()
+
+    gather_col(lambda k, piece: xg.at[rows(lax.rem(r + nr - k, nr), rd), lanes(piece)],
+               b_s, b_r, ready_x)
+    for k in range(1, nr):
+        a[k].wait_send()
+
+    left = xg[rows(c, st), :]
+    for j in range(nc // 2 + 1):
+        right = xg[rows(lax.rem(c + j, nc), st), :]
+        block = lax.dot_general(left, right, (((1,), (1,)), ((), ())), preferred_element_type=jnp.float32)
+        part[:, j * st:(j + 1) * st] = block
+        sendb[:, j * st:(j + 1) * st] = block.astype(jnp.bfloat16)
+
+    dc = {}
+    for k in range(1, nr):
+        dc[k] = to_row(sendb.at[rows(lax.rem(r + k, nr), ch), :], recvb.at[k - 1], d_s.at[k], d_r.at[k], k)
+        dc[k].start()
+
+    step = 32
+
+    def body(i, acc):
+        v = xg[rows(i, step), :].astype(jnp.float32)
+        v = v * v
+        t = acc
+        for m in range(step // 8):
+            for n in range(v.shape[1] // 128):
+                t = t + v[8 * m:8 * m + 8, 128 * n:128 * n + 128]
+        return t
+
+    ssg[0] = lax.fori_loop(0, xg.shape[0] // step, body, jnp.zeros((8, 128), jnp.float32))
+    sc = {}
+    for k in range(1, nr):
+        sc[k] = to_row(ssg.at[0], ssg.at[k], s_s.at[k], s_r.at[k], k)
+        sc[k].start()
+    xd_ref[...] = xg[:, lanes(c)]
+
+    for k in range(1, nr):
+        dc[k].wait_recv()
+    total = part[rows(r, ch), :]
+    for k in range(1, nr):
+        total = total + recvb[k - 1].astype(jnp.float32)
+    h_ref[rows(c * nr + r, ch), :] = total.astype(jnp.bfloat16)
+
+    fc = {}
+    for k in range(1, nr):
+        mine = h_ref.at[rows(c * nr + r, ch), :]
+        fc[k] = to_row(mine, mine, f_s.at[k], f_r.at[k], k)
+        fc[k].start()
+
+    def ready_h(k):
+        if k > 0:
+            fc[k].wait_recv()
+
+    gather_col(lambda k, piece: h_ref.at[rows(piece * nr + lax.rem(r + nr - k, nr), ch), :],
+               g_s, g_r, ready_h)
+    for k in range(1, nr):
+        sc[k].wait_recv()
+    tot = ssg[0]
+    for k in range(1, nr):
+        tot = tot + ssg[k]
+    ss_ref[...] = tot
+    for k in range(1, nr):
+        dc[k].wait_send()
+        sc[k].wait_send()
+        fc[k].wait_send()
+
+
+def row_gram(unfolding, nr, nc):
+    rd, cd = unfolding.shape
+    total_rows = rd * nr
+    w = cd // nr
+    st = total_rows // nc
+    half = (nc // 2 + 1) * st
+    vm = pl.BlockSpec(memory_space=pltpu.VMEM)
+    dma = pltpu.SemaphoreType.DMA
+    stripes, mine, squares = pl.pallas_call(
+        functools.partial(exchange, nr, nc),
+        out_shape=(
+            jax.ShapeDtypeStruct((total_rows, half), jnp.bfloat16),
+            jax.ShapeDtypeStruct((total_rows, w), jnp.bfloat16),
+            jax.ShapeDtypeStruct((8, 128), jnp.float32),
+        ),
+        in_specs=[vm],
+        out_specs=(vm, vm, vm),
+        scratch_shapes=[
+            pltpu.VMEM((total_rows, nc * w), jnp.bfloat16),
+            pltpu.VMEM((st, half), jnp.float32),
+            pltpu.VMEM((st, half), jnp.bfloat16),
+            pltpu.VMEM((nr - 1, st // nr, half), jnp.bfloat16),
+            pltpu.VMEM((nr, 8, 128), jnp.float32),
+            dma, dma((nr,)), dma((nr,)), dma((nr, nc)), dma((nr, nc)),
+            dma((nr,)), dma((nr,)), dma((nr,)), dma((nr,)),
+            dma((nr,)), dma((nr,)), dma((nr, nc)), dma((nr, nc)),
+        ],
+        compiler_params=pltpu.CompilerParams(
+            collective_id=0, has_side_effects=True, vmem_limit_bytes=56 * 1024 * 1024),
+    )(unfolding)
+    return stripes, mine, jnp.sum(squares)
+
+
+def expand(stripes, nc):
+    st = stripes.shape[0] // nc
+
+    def block(i, j):
+        d = (j - i) % nc
+        if d <= nc // 2:
+            return stripes[i * st:(i + 1) * st, d * st:(d + 1) * st]
+        d = (i - j) % nc
+        return stripes[j * st:(j + 1) * st, d * st:(d + 1) * st].T
+
+    return jnp.concatenate(
+        [jnp.concatenate([block(i, j) for j in range(nc)], axis=1) for i in range(nc)], axis=0)
+
+
+def local_rows(unfolding, nr, nc):
+    rd, cd = unfolding.shape
+    stripes, mine, sumsq = row_gram(unfolding, nr, nc)
+    gram = expand(stripes, nc)
+    factor = math.sqrt(COLS) / (3.0 * jnp.sqrt(sumsq))
+    square = factor * factor
+
+    def times(v):
+        return square * lax.dot_general(
+            v.astype(jnp.bfloat16), gram, (((1,), (0,)), ((), ())), preferred_element_type=jnp.float32)
+
+    def poly(v, op):
+        one = op(v)
+        return 1.875 * v - 1.25 * one + 0.375 * op(one)
+
+    def apply_op(level):
+        if level == 0:
+            return times
+        lower = apply_op(level - 1)
+        return lambda v: lower(poly(poly(v, lower), lower))
+
+    value = factor * mine.T.astype(jnp.float32)
+    for turn_index in range(ITERS):
+        value = poly(value, apply_op(turn_index))
+    final = (value * math.sqrt(rd * nr)).astype(jnp.bfloat16)
+    cols = lax.all_to_all(final, "row", split_axis=1, concat_axis=0, tiled=True)
+    cube = cols.reshape(cd // PIXELS, PIXELS, rd).transpose(1, 0, 2)
+    return lax.all_to_all(cube, "col", split_axis=0, concat_axis=1, tiled=True)
+
+
+def local_cols(unfolding):
     rows_dev = unfolding.shape[0]
     cols_dev = unfolding.shape[1]
     total_rows = rows_dev * lax.axis_size("row")
@@ -49,6 +265,15 @@
 
 
 def solution(mesh):
+    nr, nc = mesh.shape["row"], mesh.shape["col"]
+
+    def local(unfolding):
+        rd, cd = unfolding.shape
+        fits = cd % (128 * nr) == 0 and nc % 2 == 0 and (rd * nr) % (16 * nr * nc) == 0
+        if rd * nr <= cd * nc and fits:
+            return local_rows(unfolding, nr, nc)
+        return local_cols(unfolding)
+
     return jax.shard_map(
         local,
         mesh=mesh,

time: 767 us -> 437 us (0.57); the launches traced: 767 us -> 429 us
  waiting for transfers between devices: 631 us -> 0 us
  Pallas kernels: 0 us -> 146 us
  matrix products: 52.4 us -> 154 us
  local copies, waits for them, and re-layouts: 3.94 us -> 65.8 us
  between operations: 14.3 us -> 1.34 us
    all_gather x6 -> x0, waiting for transfers between devices: 342 us -> none  [the longest x2 163 us: local(): gram_rows = lax.all_gather(shares, 'row', axis=1, tiled=True)]
    reduce_scatter x2 -> x0, waiting for transfers between devices: 289 us -> none  [local(): lax.psum_scatter(partial_gram, 'row', scatter_dimension=1, tiled=True)]
    pallas_call x0 -> x1, Pallas kernels: none -> 146 us  [row_gram(): pl.pallas_call(functools.partial(exchange, nr, nc), out_shape=(jax.ShapeD...]
    dot_general x6 -> x10, matrix products: 52.4 us -> 154 us  [times(): lax.dot_general(v.astype(jnp.bfloat16), gram, (((1,), (0,)), ((), ())), p...]
    psum x1 -> x0, blocking collectives: 42.2 us -> none  [local(): sumsq = lax.psum(jnp.sum(values * values), ('row', 'col'))]
    all_to_all x1 -> x2, blocking collectives: 15.1 us -> 53.5 us  [the longest x1 38.3 us: local_rows(): cols = lax.all_to_all(final, 'row', split_axis=1, concat_axis=0, tiled=True)]
    unnamed x5 -> x30, local copies, waits for them, and re-layouts: 1.42 us -> 34.1 us
    pallas_call x0 -> x1, local copies, waits for them, and re-layouts: none -> 16.3 us  [row_gram(): pl.pallas_call(functools.partial(exchange, nr, nc), out_shape=(jax.ShapeD...]
  transfers between devices with their start and end apart: 8 -> 0, of which waited for: 8 -> 0; matrix products, arithmetic and copies ran while one was open for 0% -> 0% of each run, Pallas kernels for 0% -> 0%
where the time goes in v1:
time: 437 us; the launch traced here: 429 us
  matrix products  154 us (35%)
  Pallas kernels  146 us (33%)
  local copies, waits for them, and re-layouts  65.8 us (15%)
  blocking collectives  53.5 us (12%)
  other arithmetic  7.45 us (2%)
    dot_general x10, matrix products, times(): lax.dot_general(v.astype(jnp.bfloat16), gram, (((1,), (0,)), ((), ())), p...  154 us
    pallas_call x1, Pallas kernels, row_gram(): pl.pallas_call(functools.partial(exchange, nr, nc), out_shape=(jax.ShapeD...  146 us
    all_to_all x1, blocking collectives, local_rows(): cols = lax.all_to_all(final, 'row', split_axis=1, concat_axis=0, tiled=True)  38.3 us
    unnamed x30, local copies, waits for them, and re-layouts  34.1 us
    pallas_call x1, local copies, waits for them, and re-layouts, row_gram(): pl.pallas_call(functools.partial(exchange, nr, nc), out_shape=(jax.ShapeD...  16.3 us
    all_to_all x1, blocking collectives, local_rows(): return lax.all_to_all(cube, 'col', split_axis=0, concat_axis=1, tiled=True)  15.2 us

profile of v1, /device:TPU:0, one launch (start us, length us, event | category | flops | bytes accessed | tf_op | source)
XLA Modules:
  0.0 428.7 jit_solution(1687043491991474250)
XLA Ops:
  0.0 146.4 %shard_map.17 = (bf16[3072,1920]{1,0:T(8,128)(2,1)}, bf16[3072,128]{1,0:T(8,128)(2,1)}, f32[8,128]{1,0:T(8,128)}) custom-call(bf16[768,512]{1,0:T(8,128)(2,1)} %x_ref.1), custom_call_target="tpu_custom_call" | custom-call | tf_op jit(solution)/shard_map/pallas_call | solution.py:160
  146.4 4.7 %fusion.53 = (bf16[384,1920]{1,0:T(8,128)(2,1)S(1)}, bf16[384,1920]{1,0:T(8,128)(2,1)S(1)}, bf16[384,1920]{1,0:T(8,128)(2,1)}, bf16[384,1920]{1,0:T(8,128)(2,1)}) fusion(bf16[3072,1920]{1,0:T(8,128)(2,1)} %get-tuple-element.10), kind=kLoop, calls=%fused_computation.103 | loop fusion | bytes 11796480 | tf_op jit(solution)/shard_map/slice | solution.py:191
  151.2 0.0 copy-start.5
  151.2 16.3 %copy.110 = bf16[3072,1920]{0,1:T(8,128)(2,1)} copy(bf16[3072,1920]{1,0:T(8,128)(2,1)} %get-tuple-element.10) | data formatting | bytes 23592960 | tf_op jit(solution)/shard_map/pallas_call | solution.py:160
  167.5 0.0 copy-done.5
  167.5 0.6 reduce_sum.9
  168.8 0.0 copy-start.4
  168.8 2.5 slice_bitcast_fusion.11
  171.3 0.0 copy-done.4
  171.3 0.0 copy-start.3
  171.3 1.6 maximum_dynamic-update-slice_fusion.3
  172.9 0.4 copy-done.3
  173.3 1.7 maximum_dynamic-update-slice_fusion.2
  175.1 1.8 maximum_dynamic-update-slice_fusion.1
  176.8 1.8 maximum_dynamic-update-slice_fusion
  178.6 2.2 slice_bitcast_fusion.21
  180.8 0.2 copy.133
  181.0 0.2 copy.131
  181.2 0.2 copy.132
  181.4 1.8 fusion.46
  183.2 1.7 fusion.45
  184.9 1.7 fusion.44
  186.6 2.5 slice_dynamic-update-slice_fusion.1
  189.1 2.0 slice_dynamic-update-slice_fusion.5
  191.1 1.7 fusion.43
  192.8 1.7 fusion.42
  194.6 1.7 fusion.41
  196.3 2.2 slice_dynamic-update-slice_fusion.3
  198.6 2.2 slice_dynamic-update-slice_fusion.2
  200.8 1.7 fusion.40
  202.5 1.7 fusion.39
  204.2 1.7 fusion.38
  206.0 2.0 slice_dynamic-update-slice_fusion.4
  207.9 0.0 copy-start.2
  207.9 2.5 slice_dynamic-update-slice_fusion
  210.4 0.8 constant_dynamic-update-slice_fusion
  211.2 0.8 constant_dynamic-update-slice_fusion.1
  212.0 0.8 constant_dynamic-update-slice_fusion.2
  212.8 1.8 slice_dynamic-update-slice_fusion.6
  214.6 0.0 copy-done.2
  214.6 11.3 %convolution_multiply_fusion.11 = f32[128,3072]{0,1:T(8,128)S(1)} fusion(bf16[3072,3072]{1,0:T(8,128)(2,1)} %slice_dynamic-update-slice_fusion.6, bf16[3072,128]{1,0:T(8,128)(2,1)S(1)} %copy-done.2, f32[]{:T(128)S(6)} %mul.125, f32[]{:T(128)S(6)} %div.3), kind=kOutput, calls=%fused_computation.11 | convolution fusion | flops 2417491968 | bytes 21233672 | tf_op jit(solution)/shard_map/dot_general | solution.py:207
  225.9 11.8 %fusion.12 = f32[128,3072]{0,1:T(8,128)S(1)} fusion(bf16[3072,3072]{1,0:T(8,128)(2,1)} %slice_dynamic-update-slice_fusion.6, f32[128,3072]{0,1:T(8,128)S(1)} %convolution_multiply_fusion.11, bf16[3072,128]{1,0:T(8,128)(2,1)S(1)} %copy-done.2, f32[]{:T(128)S(6)} %mul.125, f32[]{:T(128)S(6)} %div.3), kind=kOutput, calls=%fused_computation.24 | convolution fusion | flops 2419458048 | bytes 22806536 | tf_op jit(solution)/shard_map/dot_general | solution.py:207
  237.6 11.4 %convolution_multiply_fusion.9 = f32[128,3072]{0,1:T(8,128)S(1)} fusion(bf16[3072,3072]{1,0:T(8,128)(2,1)} %slice_dynamic-update-slice_fusion.6, f32[128,3072]{0,1:T(8,128)S(1)} %fusion.12, f32[]{:T(128)S(6)} %mul.125), kind=kOutput, calls=%fused_computation.9 | convolution fusion | flops 2416705536 | bytes 22020100 | tf_op jit(solution)/shard_map/dot_general | solution.py:207
  249.1 11.5 %fusion.11 = f32[128,3072]{0,1:T(8,128)S(1)} fusion(bf16[3072,3072]{1,0:T(8,128)(2,1)} %slice_dynamic-update-slice_fusion.6, f32[128,3072]{0,1:T(8,128)S(1)} %convolution_multiply_fusion.9, f32[128,3072]{0,1:T(8,128)S(1)} %fusion.12, f32[]{:T(128)S(6)} %mul.125), kind=kOutput, calls=%fused_computation.23 | convolution fusion | flops 2418671616 | bytes 23592964 | tf_op jit(solution)/shard_map/dot_general | solution.py:207
  260.6 0.0 copy-start.1
  260.6 1.1 copy-done.1
  261.7 12.7 %convolution_multiply_fusion.7 = f32[128,3072]{0,1:T(8,128)} fusion(bf16[3072,3072]{1,0:T(8,128)(2,1)} %slice_dynamic-update-slice_fusion.6, f32[128,3072]{0,1:T(8,128)S(1)} %fusion.11, f32[]{:T(128)S(6)} %mul.125), kind=kOutput, calls=%fused_computation.7 | convolution fusion | flops 2416705536 | bytes 22020100 | tf_op jit(solution)/shard_map/dot_general | solution.py:207
  274.4 29.2 %convolution_multiply_fusion.5 = f32[128,3072]{0,1:T(8,128)S(1)} fusion(bf16[3072,3072]{1,0:T(8,128)(2,1)} %slice_dynamic-update-slice_fusion.6, f32[128,3072]{0,1:T(8,128)} %convolution_multiply_fusion.7, f32[128,3072]{0,1:T(8,128)} %copy-done.1, f32[]{:T(128)S(6)} %mul.125), kind=kOutput, calls=%fused_computation.5 | convolution fusion | flops 4835377152 | bytes 23592964 | tf_op jit(solution)/shard_map/dot_general | solution.py:207
  303.6 11.6 %convolution_multiply_fusion.4 = f32[128,3072]{0,1:T(8,128)S(1)} fusion(bf16[3072,3072]{1,0:T(8,128)(2,1)} %slice_dynamic-update-slice_fusion.6, f32[128,3072]{0,1:T(8,128)S(1)} %convolution_multiply_fusion.5, f32[]{:T(128)S(6)} %mul.125), kind=kOutput, calls=%fused_computation.4 | convolution fusion | flops 2416705536 | bytes 22020100 | tf_op jit(solution)/shard_map/dot_general | solution.py:207
  315.3 11.5 %fusion.9 = f32[128,3072]{0,1:T(8,128)S(1)} fusion(bf16[3072,3072]{1,0:T(8,128)(2,1)} %slice_dynamic-update-slice_fusion.6, f32[128,3072]{0,1:T(8,128)S(1)} %convolution_multiply_fusion.4, f32[128,3072]{0,1:T(8,128)S(1)} %convolution_multiply_fusion.5, f32[]{:T(128)S(6)} %mul.125), kind=kOutput, calls=%fused_computation.21 | convolution fusion | flops 2418671616 | bytes 23592964 | tf_op jit(solution)/shard_map/dot_general | solution.py:207
  326.8 0.0 copy-start
  326.8 1.1 copy-done
  327.9 12.5 %convolution_multiply_fusion.2 = f32[128,3072]{0,1:T(8,128)} fusion(bf16[3072,3072]{1,0:T(8,128)(2,1)} %slice_dynamic-update-slice_fusion.6, f32[128,3072]{0,1:T(8,128)S(1)} %fusion.9, f32[]{:T(128)S(6)} %mul.125), kind=kOutput, calls=%fused_computation.2 | convolution fusion | flops 2416705536 | bytes 22020100 | tf_op jit(solution)/shard_map/dot_general | solution.py:207
  340.4 30.6 %fusion.13 = bf16[128,3072]{0,1:T(8,128)(2,1)} fusion(bf16[3072,3072]{1,0:T(8,128)(2,1)} %slice_dynamic-update-slice_fusion.6, f32[128,3072]{0,1:T(8,128)S(1)} %convolution_multiply_fusion.5, f32[128,3072]{0,1:T(8,128)} %convolution_multiply_fusion.2, f32[128,3072]{0,1:T(8,128)} %copy-done, f32[128,3072]{0,1:T(8,128)S(1)} %fusion.12, f32[]{:T(128)S(6)} %mul.125), kind=kOutput, calls=%fused_computation.25 | convolution fusion | flops 4838129664 | bytes 25952260 | tf_op jit(solution)/shard_map/dot_general | solution.py:207
  371.1 1.4 copy.146
  372.5 38.3 %all_to_all.34 = bf16[128,4,768]{2,0,1:T(8,128)(2,1)S(1)} all-to-all(bf16[128,4,768]{2,0,1:T(8,128)(2,1)S(1)} %copy.146), channel_id=1, replica_groups=mesh['row'=4,'col'=8] {'row'}, dimensions={1} | all-to-all | bytes 1572864 | tf_op jit(solution)/shard_map/all_to_all | solution.py:224
  410.8 0.8 copy.147
  411.6 15.2 %all_to_all.35 = bf16[256,2,768]{2,1,0:T(2,128)(2,1)S(1)} all-to-all(bf16[256,2,768]{2,1,0:T(2,128)(2,1)S(1)} %copy.147), channel_id=1, replica_groups=mesh['row'=4,'col'=8] {'col'}, dimensions={0} | all-to-all | bytes 1572864 | tf_op jit(solution)/shard_map/all_to_all | solution.py:226
  426.8 0.1 copy.148
  426.9 0.1 copy.149
  426.9 1.3 copy.150
Async XLA Ops:
  151.2 16.3 %copy-start.5 = (f32[8,128]{1,0:T(8,128)S(1)}, f32[8,128]{1,0:T(8,128)}, u32[]{:S(2)}) copy-start(f32[8,128]{1,0:T(8,128)} %get-tuple-element.8) | copy-start | bytes 12292
  168.8 2.5 copy-start.4
  171.3 2.0 copy-start.3
  207.9 6.6 %copy-start.2 = (bf16[3072,128]{1,0:T(8,128)(2,1)S(1)}, bf16[3072,128]{1,0:T(8,128)(2,1)}, u32[]{:S(2)}) copy-start(bf16[3072,128]{1,0:T(8,128)(2,1)} %get-tuple-element.9) | copy-start | bytes 2359300
  260.6 1.1 copy-start.1
  326.8 1.1 copy-start

commit v2 on v1

--- a/solution.py
+++ b/solution.py
@@ -14,8 +14,8 @@
 MESH = pl.DeviceIdType.MESH
 
 
-def exchange(nr, nc, x_ref, h_ref, xd_ref, ss_ref, xg, part, sendb, recvb, ssg,
-             own_sem, a_s, a_r, b_s, b_r, d_s, d_r, s_s, s_r, f_s, f_r, g_s, g_r):
+def exchange(nr, nc, x_ref, out_ref, h_ref, xg, part, sendb, recvb, ssg, full, floats, halves, turned,
+             own_sem, a_s, a_r, b_s, b_r, d_s, d_r, s_s, s_r, f_s, f_r, g_s, g_r, o_s, o_r):
     r = lax.axis_index("row")
     c = lax.axis_index("col")
     rd = x_ref.shape[0]
@@ -25,11 +25,12 @@
     direct = tuple(range(2, nc, 2))
 
     barrier = pltpu.get_barrier_semaphore()
-    for k in range(1, nr):
-        pl.semaphore_signal(barrier, inc=1, device_id=(lax.rem(r + k, nr), c), device_id_type=MESH)
-    for d in (1,) + direct:
-        pl.semaphore_signal(barrier, inc=1, device_id=(r, c ^ d), device_id_type=MESH)
-    pl.semaphore_wait(barrier, nr - 1 + 1 + len(direct))
+    for k in range(nr):
+        for m in range(nc):
+            if k or m:
+                pl.semaphore_signal(
+                    barrier, inc=1, device_id=(lax.rem(r + k, nr), lax.rem(c + m, nc)), device_id_type=MESH)
+    pl.semaphore_wait(barrier, nr * nc - 1)
 
     def lanes(index):
         return pl.ds(pl.multiple_of(index * w, w), w)
@@ -47,7 +48,7 @@
             src_ref=src, dst_ref=dst, send_sem=s_sem, recv_sem=r_sem,
             device_id=(r, c ^ d), device_id_type=MESH)
 
-    def gather_col(view, s_sem, r_sem, ready):
+    def gather_col(view, s_sem, r_sem, ready, landed):
         copies = {}
 
         def send(k, piece, slot, d):
@@ -63,9 +64,11 @@
             for d in direct:
                 copies[k, d].wait_recv()
                 send(k, c ^ d, d ^ 1, 1)
-        for k in range(nr):
-            for d in range(1, nc, 2):
-                copies[k, d].wait_recv()
+        for d in (0,) + direct + tuple(range(1, nc, 2)):
+            if d % 2:
+                for k in range(nr):
+                    copies[k, d].wait_recv()
+            landed(c ^ d)
         for key in copies:
             copies[key].wait_send()
 
@@ -84,7 +87,7 @@
             a[k].wait_recv()
 
     gather_col(lambda k, piece: xg.at[rows(lax.rem(r + nr - k, nr), rd), lanes(piece)],
-               b_s, b_r, ready_x)
+               b_s, b_r, ready_x, lambda piece: None)
     for k in range(1, nr):
         a[k].wait_send()
 
@@ -116,8 +119,6 @@
     for k in range(1, nr):
         sc[k] = to_row(ssg.at[0], ssg.at[k], s_s.at[k], s_r.at[k], k)
         sc[k].start()
-    xd_ref[...] = xg[:, lanes(c)]
-
     for k in range(1, nr):
         dc[k].wait_recv()
     total = part[rows(r, ch), :]
@@ -135,95 +136,179 @@
         if k > 0:
             fc[k].wait_recv()
 
+    half = nc // 2
+
+    def mirror(i):
+        def turn(index, carry):
+            d, t = index // (st // 128), lax.rem(index, st // 128)
+            j = lax.rem(i + d, nc)
+            piece = h_ref[pl.ds(pl.multiple_of(i * st + t * 128, 128), 128), lanes_of(d * st, st)]
+            full[rows(j, st), lanes_of(i * st + t * 128, 128)] = piece.T
+            return carry
+
+        def keep(d, carry):
+            full[rows(i, st), lanes_of(lax.rem(i + d, nc) * st, st)] = h_ref[rows(i, st), lanes_of(d * st, st)]
+            return carry
+
+        lax.fori_loop(0, half + 1, keep, 0)
+        lax.fori_loop(st // 128, half * (st // 128), turn, 0)
+
+    def lanes_of(start, size):
+        return pl.ds(pl.multiple_of(start, 128), size)
+
     gather_col(lambda k, piece: h_ref.at[rows(piece * nr + lax.rem(r + nr - k, nr), ch), :],
-               g_s, g_r, ready_h)
+               g_s, g_r, ready_h, mirror)
     for k in range(1, nr):
         sc[k].wait_recv()
     tot = ssg[0]
     for k in range(1, nr):
         tot = tot + ssg[k]
-    ss_ref[...] = tot
     for k in range(1, nr):
         dc[k].wait_send()
         sc[k].wait_send()
         fc[k].wait_send()
 
-
-def row_gram(unfolding, nr, nc):
+    sumsq = jnp.full((8, 128), jnp.sum(tot), jnp.float32)
+    factor = (math.sqrt(w * nr * nc) / (3.0 * jnp.sqrt(sumsq)))[0:1, :]
+    square = factor * factor
+
+    def product(src, emit):
+        def tile(m, carry):
+            at = rows(m, st)
+            emit(at, square * jnp.dot(full[at, :], halves[src], preferred_element_type=jnp.float32))
+            return carry
+
+        lax.fori_loop(0, nc, tile, 0)
+
+    def store(slot):
+        def emit(at, value):
+            floats[slot, at, :] = value
+            halves[slot, at, :] = value.astype(jnp.bfloat16)
+        return emit
+
+    def poly(src, temp, dst):
+        product(src, store(temp))
+        product(temp, lambda at, two: store(dst)(
+            at, 1.875 * floats[src, at, :] - 1.25 * floats[temp, at, :] + 0.375 * two))
+
+    def begin(m, carry):
+        store(0)(rows(m, st), factor * xg[rows(m, st), lanes(c)].astype(jnp.float32))
+        return carry
+
+    lax.fori_loop(0, nc, begin, 0)
+    poly(0, 1, 2)
+
+    def follow(m, carry):
+        floats[4, rows(m, st), :] = 1.875 * floats[2, rows(m, st), :]
+        return carry
+
+    lax.fori_loop(0, nc, follow, 0)
+
+    def level(turn_index, carry):
+        weight = jnp.where(turn_index == 0, -1.25, 0.375)
+        poly(2, 1, 0)
+        poly(0, 1, 3)
+
+        def emit(at, value):
+            halves[2, at, :] = value.astype(jnp.bfloat16)
+            floats[2, at, :] = value
+            floats[4, at, :] += weight * value
+
+        product(3, emit)
+        return carry
+
+    lax.fori_loop(0, 2, level, 0)
+
+    scale = math.sqrt(xg.shape[0])
+
+    def flip(m, carry):
+        piece = (scale * floats[4, pl.ds(pl.multiple_of(m * 128, 128), 128), :]).T
+        turned[m // (rd // 128), :, lanes_of(lax.rem(m, rd // 128) * 128, 128)] = piece.astype(jnp.bfloat16)
+        return carry
+
+    lax.fori_loop(0, nr * rd // 128, flip, 0)
+
+    first_col = (c * nr + r) * w
+    qd = PIXELS // nc
+    share = w // qd
+    view = first_col // PIXELS
+    base = lax.rem(first_col, PIXELS) // qd
+    copies = []
+    for k in range(nr):
+        for t in range(share):
+            to = lax.rem(r + k, nr)
+            src = turned.at[to, pl.ds(t * qd, qd), :]
+            dst = out_ref.at[view]
+            copy = pltpu.make_async_remote_copy(
+                src_ref=src, dst_ref=dst, send_sem=o_s.at[k * share + t], recv_sem=o_r.at[view],
+                device_id=(to, base + t), device_id_type=MESH)
+            if k:
+                copy.start()
+                copies.append((None, copy))
+            else:
+                other = base + t != c
+
+                @pl.when(other)
+                def _(copy=copy):
+                    copy.start()
+
+                @pl.when(jnp.logical_not(other))
+                def _(src=src, dst=dst):
+                    mine = pltpu.make_async_copy(src, dst, own_sem)
+                    mine.start()
+                    mine.wait()
+
+                copies.append((other, copy))
+    for v in range(out_ref.shape[0]):
+        source = (v * PIXELS + (c * qd // w) * w) // w
+        away = source != c * nr + r
+
+        @pl.when(away)
+        def _(v=v):
+            pltpu.make_async_remote_copy(
+                src_ref=turned.at[0, pl.ds(0, qd), :], dst_ref=out_ref.at[v], send_sem=o_s.at[0],
+                recv_sem=o_r.at[v], device_id=(lax.rem(r + 1, nr), c), device_id_type=MESH).wait_recv()
+    for other, copy in copies:
+        if other is None:
+            copy.wait_send()
+        else:
+            pl.when(other)(lambda copy=copy: copy.wait_send())
+
+
+def local_rows(unfolding, nr, nc):
     rd, cd = unfolding.shape
     total_rows = rd * nr
     w = cd // nr
     st = total_rows // nc
     half = (nc // 2 + 1) * st
+    views = cd * nc // PIXELS
     vm = pl.BlockSpec(memory_space=pltpu.VMEM)
     dma = pltpu.SemaphoreType.DMA
-    stripes, mine, squares = pl.pallas_call(
+    blocks = pl.pallas_call(
         functools.partial(exchange, nr, nc),
-        out_shape=(
-            jax.ShapeDtypeStruct((total_rows, half), jnp.bfloat16),
-            jax.ShapeDtypeStruct((total_rows, w), jnp.bfloat16),
-            jax.ShapeDtypeStruct((8, 128), jnp.float32),
-        ),
+        out_shape=jax.ShapeDtypeStruct((views, PIXELS // nc, rd), jnp.bfloat16),
         in_specs=[vm],
-        out_specs=(vm, vm, vm),
+        out_specs=vm,
         scratch_shapes=[
+            pltpu.VMEM((total_rows, half), jnp.bfloat16),
             pltpu.VMEM((total_rows, nc * w), jnp.bfloat16),
             pltpu.VMEM((st, half), jnp.float32),
             pltpu.VMEM((st, half), jnp.bfloat16),
             pltpu.VMEM((nr - 1, st // nr, half), jnp.bfloat16),
             pltpu.VMEM((nr, 8, 128), jnp.float32),
+            pltpu.VMEM((total_rows, total_rows), jnp.bfloat16),
+            pltpu.VMEM((5, total_rows, w), jnp.float32),
+            pltpu.VMEM((4, total_rows, w), jnp.bfloat16),
+            pltpu.VMEM((nr, w, rd), jnp.bfloat16),
             dma, dma((nr,)), dma((nr,)), dma((nr, nc)), dma((nr, nc)),
             dma((nr,)), dma((nr,)), dma((nr,)), dma((nr,)),
             dma((nr,)), dma((nr,)), dma((nr, nc)), dma((nr, nc)),
+            dma((nr * nc,)), dma((views,)),
         ],
         compiler_params=pltpu.CompilerParams(
-            collective_id=0, has_side_effects=True, vmem_limit_bytes=56 * 1024 * 1024),
+            collective_id=0, has_side_effects=True, vmem_limit_bytes=63 * 1024 * 1024),
     )(unfolding)
-    return stripes, mine, jnp.sum(squares)
-
-
-def expand(stripes, nc):
-    st = stripes.shape[0] // nc
-
-    def block(i, j):
-        d = (j - i) % nc
-        if d <= nc // 2:
-            return stripes[i * st:(i + 1) * st, d * st:(d + 1) * st]
-        d = (i - j) % nc
-        return stripes[j * st:(j + 1) * st, d * st:(d + 1) * st].T
-
-    return jnp.concatenate(
-        [jnp.concatenate([block(i, j) for j in range(nc)], axis=1) for i in range(nc)], axis=0)
-
-
-def local_rows(unfolding, nr, nc):
-    rd, cd = unfolding.shape
-    stripes, mine, sumsq = row_gram(unfolding, nr, nc)
-    gram = expand(stripes, nc)
-    factor = math.sqrt(COLS) / (3.0 * jnp.sqrt(sumsq))
-    square = factor * factor
-
-    def times(v):
-        return square * lax.dot_general(
-            v.astype(jnp.bfloat16), gram, (((1,), (0,)), ((), ())), preferred_element_type=jnp.float32)
-
-    def poly(v, op):
-        one = op(v)
-        return 1.875 * v - 1.25 * one + 0.375 * op(one)
-
-    def apply_op(level):
-        if level == 0:
-            return times
-        lower = apply_op(level - 1)
-        return lambda v: lower(poly(poly(v, lower), lower))
-
-    value = factor * mine.T.astype(jnp.float32)
-    for turn_index in range(ITERS):
-        value = poly(value, apply_op(turn_index))
-    final = (value * math.sqrt(rd * nr)).astype(jnp.bfloat16)
-    cols = lax.all_to_all(final, "row", split_axis=1, concat_axis=0, tiled=True)
-    cube = cols.reshape(cd // PIXELS, PIXELS, rd).transpose(1, 0, 2)
-    return lax.all_to_all(cube, "col", split_axis=0, concat_axis=1, tiled=True)
+    return blocks.transpose(1, 0, 2)
 
 
 def local_cols(unfolding):
@@ -269,7 +354,9 @@
 
     def local(unfolding):
         rd, cd = unfolding.shape
-        fits = cd % (128 * nr) == 0 and nc % 2 == 0 and (rd * nr) % (16 * nr * nc) == 0
+        w = cd // nr
+        fits = w == 128 and cd % (128 * nr) == 0 and nc % 2 == 0 and (rd * nr) % (128 * nc) == 0
+        fits = fits and PIXELS % w == 0 and w % (PIXELS // nc) == 0 and rd % 128 == 0 and ITERS == 2
         if rd * nr <= cd * nc and fits:
             return local_rows(unfolding, nr, nc)
         return local_cols(unfolding)

time: 437 us -> 257 us (0.59)
  matrix products: 154 us -> 0 us
  Pallas kernels: 146 us -> 250 us
  local copies, waits for them, and re-layouts: 65.8 us -> 2.45 us
  blocking collectives: 53.5 us -> 0 us
  other arithmetic: 7.45 us -> 0 us
    dot_general x10 -> x0, matrix products: 154 us -> none  [times(): lax.dot_general(v.astype(jnp.bfloat16), gram, (((1,), (0,)), ((), ())), p...]
    pallas_call x1, Pallas kernels: 146 us -> 250 us  [local_rows(): pl.pallas_call(functools.partial(exchange, nr, nc), out_shape=jax.ShapeDt...]
    all_to_all x2 -> x0, blocking collectives: 53.5 us -> none  [the longest x1 38.3 us: local_rows(): cols = lax.all_to_all(final, 'row', split_axis=1, concat_axis=0, tiled=True)]
    unnamed x30 -> x0, local copies, waits for them, and re-layouts: 34.1 us -> none
    pallas_call x1 -> x0, local copies, waits for them, and re-layouts: 16.3 us -> none  [row_gram(): pl.pallas_call(functools.partial(exchange, nr, nc), out_shape=(jax.ShapeD...]
    unnamed x4 -> x0, other arithmetic: 6.85 us -> none
    slice x1 -> x0, local copies, waits for them, and re-layouts: 4.74 us -> none  [block(): return stripes[i * st:(i + 1) * st, d * st:(d + 1) * st]]
where the time goes in v2:
time: 257 us; the launch traced here: 253 us
  Pallas kernels  250 us (97%)
    pallas_call x1, Pallas kernels, local_rows(): pl.pallas_call(functools.partial(exchange, nr, nc), out_shape=jax.ShapeDt...  250 us

profile of v2, /device:TPU:0, one launch (start us, length us, event | category | flops | bytes accessed | tf_op | source)
XLA Modules:
  0.0 252.8 jit_solution(10026613567194776590)
XLA Ops:
  0.0 250.3 %shard_map.17 = bf16[16,32,768]{2,1,0:T(8,128)(2,1)} custom-call(bf16[768,512]{1,0:T(8,128)(2,1)} %x_ref.1), custom_call_target="tpu_custom_call" | custom-call | tf_op jit(solution)/shard_map/pallas_call | solution.py:287
  250.3 2.4 copy.2

commit v3 on v2

--- a/solution.py
+++ b/solution.py
@@ -22,7 +22,6 @@
     w = x_ref.shape[1] // nr
     st = part.shape[0]
     ch = st // nr
-    direct = tuple(range(2, nc, 2))
 
     barrier = pltpu.get_barrier_semaphore()
     for k in range(nr):
@@ -51,20 +50,39 @@
     def gather_col(view, s_sem, r_sem, ready, landed):
         copies = {}
 
-        def send(k, piece, slot, d):
+        def send(k, piece, slot, d, part=None):
             ref = view(k, piece)
+            if part is not None:
+                size = ref.shape[0] // 2
+                ref = ref.at[pl.ds(part * size, size), :]
             copies[k, slot] = to_col(ref, ref, s_sem.at[k, slot], r_sem.at[k, slot], d)
             copies[k, slot].start()
 
+        def relay(k):
+            copies[k, 2].wait_recv()
+            send(k, c ^ 2, 6, 4, 0)
+            send(k, c ^ 2, 3, 1)
+            copies[k, 4].wait_recv()
+            send(k, c ^ 4, 0, 2, 1)
+            send(k, c ^ 4, 5, 1)
+
+        def relay_far(k):
+            copies[k, 6].wait_recv()
+            copies[k, 0].wait_recv()
+            send(k, c ^ 6, 7, 1)
+
         for k in range(nr):
             ready(k)
-            for d in direct + (1,):
+            for d in (2, 4, 1):
                 send(k, c, d, d)
-        for k in range(nr):
-            for d in direct:
-                copies[k, d].wait_recv()
-                send(k, c ^ d, d ^ 1, 1)
-        for d in (0,) + direct + tuple(range(1, nc, 2)):
+            if k:
+                relay(k - 1)
+            if k > 1:
+                relay_far(k - 2)
+        relay(nr - 1)
+        for k in range(max(nr - 2, 0), nr):
+            relay_far(k)
+        for d in (0, 2, 4, 6, 1, 3, 5, 7):
             if d % 2:
                 for k in range(nr):
                     copies[k, d].wait_recv()
@@ -355,7 +373,7 @@
     def local(unfolding):
         rd, cd = unfolding.shape
         w = cd // nr
-        fits = w == 128 and cd % (128 * nr) == 0 and nc % 2 == 0 and (rd * nr) % (128 * nc) == 0
+        fits = w == 128 and cd % (128 * nr) == 0 and nc == 8 and rd % 32 == 0 and (rd * nr) % (128 * nc) == 0 and (rd // nc) % 32 == 0
         fits = fits and PIXELS % w == 0 and w % (PIXELS // nc) == 0 and rd % 128 == 0 and ITERS == 2
         if rd * nr <= cd * nc and fits:
             return local_rows(unfolding, nr, nc)

time: 257 us -> 247 us (0.961)
  the two profiles are of different devices: /device:TPU:0 before, /device:TPU:11 now
where the time goes in v3:
time: 247 us
  Pallas kernels  245 us (99%)
    pallas_call x1, Pallas kernels, local_rows(): pl.pallas_call(functools.partial(exchange, nr, nc), out_shape=jax.ShapeDt...  245 us

profile of v3, /device:TPU:11, one launch (start us, length us, event | category | flops | bytes accessed | tf_op | source)
XLA Modules:
  0.0 247.0 jit_solution(16512787676855488778)
XLA Ops:
  0.0 244.6 %shard_map.17 = bf16[16,32,768]{2,1,0:T(8,128)(2,1)} custom-call(bf16[768,512]{1,0:T(8,128)(2,1)} %x_ref.1), custom_call_target="tpu_custom_call" | custom-call | tf_op jit(solution)/shard_map/pallas_call | solution.py:305
  244.6 2.4 copy.2
